TPU v7x, 32 devices: a whole 2x2x4 slice. The times are simulated.
32 devices in a mesh: rep: 4 (over z), fsdp: 2 (over x), seq: 4 (over y, core).
Axes of the slice: x: 2, y: 2, z: 4, core: 2. Of those that a mesh axis runs over, the one named last changes fastest.
Arguments:
- tokens: bfloat16 [8, 1024, 640], P(('rep', 'fsdp'), 'seq'), may hold values from -6 to 6
- d_out: bfloat16 [8, 1024, 640], P(('rep', 'fsdp'), 'seq'), may hold values from -6 to 6
- doc_lengths: int32 [8, 3], P(('rep', 'fsdp')), may hold values from 1 to 640, 1024 in all within a row
- w_query: bfloat16 [640, 1024], P('fsdp'), may hold values from -0.25 to 0.25
- w_key: bfloat16 [640, 256], P('fsdp'), may hold values from -0.25 to 0.25
- w_value: bfloat16 [640, 256], P('fsdp'), may hold values from -0.25 to 0.25
- w_out: bfloat16 [1024, 640], P('fsdp'), may hold values from -0.1875 to 0.1875
- w_gate: bfloat16 [640, 2048], P('fsdp'), may hold values from -0.25 to 0.25
- w_up: bfloat16 [640, 2048], P('fsdp'), may hold values from -0.25 to 0.25
- w_down: bfloat16 [2048, 640], P('fsdp'), may hold values from -0.125 to 0.125
- g_input: bfloat16 [640], P('fsdp'), may hold values from 0.5 to 1.5
- g_query: bfloat16 [256], P('fsdp'), may hold values from 0.25 to 1.75
- g_key: bfloat16 [256], P('fsdp'), may hold values from 0.25 to 1.75
- g_attn: bfloat16 [640], P('fsdp'), may hold values from 0.5 to 1.5
- g_ffin: bfloat16 [640], P('fsdp'), may hold values from 0.5 to 1.5
- g_ffout: bfloat16 [640], P('fsdp'), may hold values from 0.5 to 1.5
Outputs:
- result: bfloat16 [8, 1024, 640], P(('rep', 'fsdp'), 'seq')
- d_tokens: bfloat16 [8, 1024, 640], P(('rep', 'fsdp'), 'seq')
- grad_query: float32 [640, 1024], P('fsdp')
- grad_key: float32 [640, 256], P('fsdp')
- grad_value: float32 [640, 256], P('fsdp')
- grad_out: float32 [1024, 640], P('fsdp')
- grad_gate: float32 [640, 2048], P('fsdp')
- grad_up: float32 [640, 2048], P('fsdp')
- grad_down: float32 [2048, 640], P('fsdp')
- grad_ginput: float32 [640], P('fsdp')
- grad_gquery: float32 [256], P('fsdp')
- grad_gkey: float32 [256], P('fsdp')
- grad_gattn: float32 [640], P('fsdp')
- grad_gffin: float32 [640], P('fsdp')
- grad_gffout: float32 [640], P('fsdp')
Inputs may be any that keep to these rules, and one draw needn't show every extreme that they name: `doc_lengths`: each row lists the lengths of the 3 documents packed in order into one sequence; a row sums to 1024 and its largest entry is 640.
All inputs are finite; a program needn't handle non-finite values.
Results may differ from a plain program's by a relative error of at most 0.024.
Values may be sent and summed in bfloat16 or wider, within the bound.
A program may use at most 128 MiB of HBM per device.

v0:
```python
import jax
import jax.numpy as jnp
from jax import lax
from jax.sharding import PartitionSpec as P

EPS = 1e-06
ROPE_BASE = 1000000.0
MASKED = -1e30


def rms_norm(values, gain_vec):
    return values * lax.rsqrt(jnp.mean(values * values, axis=-1, keepdims=True) + EPS) * gain_vec


def rotate(values, angles):
    half_width = values.shape[-1] // 2
    front_half = values[..., :half_width]
    back_half = values[..., half_width:]
    cos_part = jnp.cos(angles)
    sin_part = jnp.sin(angles)
    return jnp.concatenate(
        [
            front_half * cos_part - back_half * sin_part,
            back_half * cos_part + front_half * sin_part,
        ],
        axis=-1,
    )


def frequencies(head_size):
    return jnp.power(
        jnp.float32(ROPE_BASE), -2.0 * jnp.arange(head_size // 2, dtype=jnp.float32) / head_size
    )


def layout(lengths_row, total_len):
    doc_ends = jnp.cumsum(lengths_row)
    starts = doc_ends - lengths_row
    indices = jnp.arange(total_len, dtype=jnp.int32)
    segment = jnp.sum((indices[:, None] >= doc_ends[None, :]).astype(jnp.int32), axis=1)
    onehot = segment[:, None] == jnp.arange(lengths_row.shape[0], dtype=jnp.int32)[None, :]
    doc_begin = jnp.sum(jnp.where(onehot, starts[None, :], 0), axis=1)
    return (segment, indices - doc_begin)


def matmul(left_side, right_side):
    return jnp.dot(left_side, right_side, preferred_element_type=jnp.float32)


def times_transpose(left_side, right_side):
    return lax.dot_general(
        left_side, right_side, (((1,), (1,)), ((), ())), preferred_element_type=jnp.float32
    )


def transpose_times(left_side, right_side):
    return lax.dot_general(
        left_side, right_side, (((0,), (0,)), ((), ())), preferred_element_type=jnp.float32
    )


def gated(gate_proj, up_proj):
    return jax.nn.gelu(gate_proj, approximate=True) * up_proj


def swap(values, axis_name, bit):
    size = lax.axis_size(axis_name)
    return lax.ppermute(values, axis_name, [(i, i ^ bit) for i in range(size)])


def halve(values, axis_name, bit, dim):
    mine = lax.axis_index(axis_name) // bit % 2
    sent = lax.dynamic_index_in_dim(values, 1 - mine, dim, keepdims=False)
    kept = lax.dynamic_index_in_dim(values, mine, dim, keepdims=False)
    arrived = swap(sent, axis_name, bit)
    return (kept.astype(jnp.float32) + arrived.astype(jnp.float32)).astype(jnp.bfloat16)


def paired():
    return lax.axis_size("fsdp") == 2 and lax.axis_size("seq") == 4


def gather_rows(shard):
    if not paired():
        return lax.all_gather(shard, "fsdp", axis=0, tiled=True)
    rows = shard.shape[0] // 4
    piece = lax.dynamic_slice_in_dim(shard, lax.axis_index("seq") * rows, rows)
    other = lax.all_gather(swap(piece, "fsdp", 1), "seq", axis=0, tiled=True)
    first = lax.axis_index("fsdp") == 0
    return jnp.concatenate([jnp.where(first, shard, other), jnp.where(first, other, shard)], axis=0)


def reduce_blocks(blocks, across_first, before):
    _, _, rows, columns = blocks.shape
    part = blocks.reshape(2, 2, 2, rows, columns)
    part = halve(part, "seq", 1, 2)
    if across_first:
        part = halve(part, "fsdp", 1, 0)
        part = halve(part, "seq", 2, 0)
    else:
        part = halve(part, "seq", 2, 1)
        part = halve(part, "fsdp", 1, 0)
    if before is not None:
        part, _ = lax.optimization_barrier((part, before))
    part = lax.psum(part, "rep")
    return (lax.all_gather(part, "seq", axis=0, tiled=True).reshape(4, rows, columns), part)


def reduce_rows(grad, across_first, before):
    low = grad.astype(jnp.bfloat16)
    if not paired():
        own = lax.psum_scatter(low, "fsdp", scatter_dimension=0, tiled=True)
        return (lax.psum(own, ("rep", "seq")).astype(jnp.float32), None)
    rows, columns = low.shape
    own, last = reduce_blocks(low.reshape(2, 4, rows // 8, columns), across_first, before)
    return (own.reshape(rows // 2, columns).astype(jnp.float32), last)


def reduce_with_gains(grad, gains, before):
    width = gains.shape[1]
    rows, columns = grad.shape
    if not paired() or width > columns:
        own = lax.psum_scatter(gains.astype(jnp.bfloat16), "fsdp", scatter_dimension=0, tiled=True)
        own = lax.psum(own, ("rep", "seq")).astype(jnp.float32)
        return (reduce_rows(grad, True, before)[0], own[0])
    extra = jnp.pad(
        gains.astype(jnp.bfloat16)[:, None, None, :],
        ((0, 0), (0, 3), (0, 15), (0, columns - width)),
    )
    blocks = jnp.concatenate(
        [grad.astype(jnp.bfloat16).reshape(2, 4, rows // 8, columns), extra], axis=2
    )
    own, _ = reduce_blocks(blocks, True, before)
    matrix = own[:, : rows // 8].reshape(rows // 2, columns).astype(jnp.float32)
    return (matrix, own[0, rows // 8, :width].astype(jnp.float32))


def body(
    tokens,
    d_out,
    doc_lengths,
    w_query,
    w_key,
    w_value,
    w_out,
    w_gate,
    w_up,
    w_down,
    g_input,
    g_query,
    g_key,
    g_attn,
    g_ffin,
    g_ffout,
):
    shards = lax.axis_size("fsdp")
    gain_shards = (g_input, g_query, g_key, g_attn, g_ffin, g_ffout)
    widths = [entry.shape[0] for entry in gain_shards]
    starts = [sum(widths[:i]) for i in range(len(widths))]
    gain_rows = lax.all_gather(jnp.concatenate(gain_shards)[None], "fsdp", axis=0, tiled=True)
    gain_input, gain_query, gain_key, gain_attn, gain_ffin, gain_ffout = [
        gain_rows[:, at : at + width].reshape(-1).astype(jnp.float32)
        for at, width in zip(starts, widths)
    ]
    qkv_mat = gather_rows(jnp.concatenate([w_query, w_key, w_value], axis=1))
    out_mat = gather_rows(w_out)
    gate_up_mat = gather_rows(jnp.concatenate([w_gate, w_up], axis=1))
    down_mat = gather_rows(w_down)
    row_count = tokens.shape[1]
    head_size = gain_query.shape[0]
    query_width = w_query.shape[1]
    head_count = query_width // head_size
    ff_width = w_gate.shape[1]
    total_len = row_count * lax.axis_size("seq")
    segment, position = layout(doc_lengths[0], total_len)
    offset = lax.axis_index("seq") * row_count
    query_seg = lax.dynamic_slice_in_dim(segment, offset, row_count)
    query_pos = lax.dynamic_slice_in_dim(position, offset, row_count)
    places = offset + jnp.arange(row_count, dtype=jnp.int32)
    allowed = (query_seg[:, None] == segment[None, :]) & (
        places[:, None] >= jnp.arange(total_len, dtype=jnp.int32)[None, :]
    )
    angles = query_pos.astype(jnp.float32)[:, None] * frequencies(head_size)[None, :]
    scaling = head_size ** (-0.5)
    inputs = tokens[0].astype(jnp.float32)
    cotangent = d_out[0].astype(jnp.float32)
    input_norm, input_pull = jax.vjp(rms_norm, inputs, gain_input)
    attn_input = input_norm.astype(jnp.bfloat16)
    qkv_proj = matmul(attn_input, qkv_mat)
    q_proj = qkv_proj[:, :query_width]
    k_proj = qkv_proj[:, query_width : query_width + head_size]
    v_proj = qkv_proj[:, query_width + head_size :]

    def query_fn(projected, gain_vec):
        shaped = projected.reshape(projected.shape[0], -1, gain_vec.shape[0])
        return rotate(rms_norm(shaped, gain_vec), angles[:, None, :])

    def key_fn(projected, gain_vec):
        return rotate(rms_norm(projected, gain_vec), angles)

    queries, query_pull = jax.vjp(query_fn, q_proj, gain_query)
    keys_own, key_pull = jax.vjp(key_fn, k_proj, gain_key)
    query_rows = queries.astype(jnp.bfloat16).reshape(row_count * head_count, head_size)
    key_value_rows = lax.all_gather(
        jnp.concatenate([keys_own.astype(jnp.bfloat16), v_proj.astype(jnp.bfloat16)], axis=1),
        "seq",
        axis=0,
        tiled=True,
    )
    key_rows = key_value_rows[:, :head_size]
    value_rows = key_value_rows[:, head_size:]

    def masked_scores():
        raw_scores = times_transpose(query_rows, key_rows).reshape(row_count, head_count, total_len)
        return jnp.where(allowed[:, None, :], raw_scores * scaling, MASKED)

    scores = masked_scores()
    top_score = jnp.max(scores, axis=-1, keepdims=True)
    shifted = jnp.exp(scores - top_score)
    denominator = jnp.sum(shifted, axis=-1, keepdims=True)
    log_total = top_score + jnp.log(denominator)
    probs_low = (
        (shifted / denominator).astype(jnp.bfloat16).reshape(row_count * head_count, total_len)
    )
    mixed_rows = (
        matmul(probs_low, value_rows)
        .reshape(row_count, head_count * head_size)
        .astype(jnp.bfloat16)
    )
    out_proj = matmul(mixed_rows, out_mat)
    attn_norm, attn_pull = jax.vjp(rms_norm, out_proj, gain_attn)
    hidden_one = inputs + attn_norm
    ffin_norm, ffin_pull = jax.vjp(rms_norm, hidden_one, gain_ffin)
    ff_input = ffin_norm.astype(jnp.bfloat16)
    gate_up_proj = matmul(ff_input, gate_up_mat)
    gate_proj = gate_up_proj[:, :ff_width]
    up_proj = gate_up_proj[:, ff_width:]
    activated, gated_pull = jax.vjp(gated, gate_proj, up_proj)
    hidden = activated.astype(jnp.bfloat16)
    down_proj = matmul(hidden, down_mat)
    ffout_norm, ffout_pull = jax.vjp(rms_norm, down_proj, gain_ffout)
    result = hidden_one + ffout_norm
    d_down, grad_gffout = ffout_pull(cotangent)
    d_down_low = d_down.astype(jnp.bfloat16)
    total_down, last = reduce_rows(transpose_times(hidden, d_down_low), True, None)
    d_hidden = times_transpose(d_down_low, down_mat)
    d_gate, d_up = gated_pull(d_hidden)
    d_gate_up_low = jnp.concatenate(
        [d_gate.astype(jnp.bfloat16), d_up.astype(jnp.bfloat16)], axis=1
    )
    total_gate_up, last = reduce_rows(transpose_times(ff_input, d_gate_up_low), False, last)
    d_ffin = times_transpose(d_gate_up_low, gate_up_mat)
    d_hidden_part, grad_gffin = ffin_pull(d_ffin)
    d_hidden_one = cotangent + d_hidden_part
    d_out_proj, grad_gattn = attn_pull(d_hidden_one)
    d_out_low = d_out_proj.astype(jnp.bfloat16)
    total_out, last = reduce_rows(transpose_times(mixed_rows, d_out_low), True, last)
    d_mixed = (
        times_transpose(d_out_low, out_mat)
        .astype(jnp.bfloat16)
        .reshape(row_count * head_count, head_size)
    )
    probs_full = jnp.exp(masked_scores() - log_total)
    d_probs = times_transpose(d_mixed, value_rows).reshape(row_count, head_count, total_len)
    row_dot = jnp.sum(probs_full * d_probs, axis=-1, keepdims=True)
    d_raw = (
        (probs_full * (d_probs - row_dot) * scaling)
        .astype(jnp.bfloat16)
        .reshape(row_count * head_count, total_len)
    )
    grad_rows = jnp.concatenate(
        [
            transpose_times(d_raw, query_rows).astype(jnp.bfloat16),
            transpose_times(probs_low, d_mixed).astype(jnp.bfloat16),
        ],
        axis=1,
    )
    d_queries = matmul(d_raw, key_rows).reshape(row_count, head_count, head_size)
    if paired():
        grad_own = grad_rows.reshape(2, 2, row_count, 2 * head_size)
        grad_own = halve(halve(grad_own, "seq", 1, 1), "seq", 2, 0).astype(jnp.float32)
    else:
        grad_own = lax.psum_scatter(grad_rows, "seq", scatter_dimension=0, tiled=True).astype(
            jnp.float32
        )
    d_q_proj, grad_gquery = query_pull(d_queries)
    d_k_proj, grad_gkey = key_pull(grad_own[:, :head_size])
    d_qkv_low = jnp.concatenate(
        [
            d_q_proj.astype(jnp.bfloat16),
            d_k_proj.astype(jnp.bfloat16),
            grad_own[:, head_size:].astype(jnp.bfloat16),
        ],
        axis=1,
    )
    d_qkv_low, last, total_down = lax.optimization_barrier((d_qkv_low, last, total_down))
    grad_qkv = transpose_times(attn_input, d_qkv_low)
    d_attn_input = times_transpose(d_qkv_low, qkv_mat)
    d_inputs_part, grad_ginput = input_pull(d_attn_input)
    d_inputs = d_hidden_one + d_inputs_part
    grad_gains = (grad_ginput, grad_gquery, grad_gkey, grad_gattn, grad_gffin, grad_gffout)
    packed_gains = jnp.concatenate([entry.reshape(shards, -1) for entry in grad_gains], axis=1)
    total_qkv, total_gains = reduce_with_gains(grad_qkv, packed_gains, last)
    return (
        result.astype(jnp.bfloat16)[None],
        d_inputs.astype(jnp.bfloat16)[None],
        total_qkv[:, :query_width],
        total_qkv[:, query_width : query_width + head_size],
        total_qkv[:, query_width + head_size :],
        total_out,
        total_gate_up[:, :ff_width],
        total_gate_up[:, ff_width:],
        total_down,
    ) + tuple((total_gains[at : at + width] for at, width in zip(starts, widths)))


def solution(mesh):
    in_specs = (
        P(("rep", "fsdp"), "seq", None),
        P(("rep", "fsdp"), "seq", None),
        P(("rep", "fsdp"), None),
        P("fsdp", None),
        P("fsdp", None),
        P("fsdp", None),
        P("fsdp", None),
        P("fsdp", None),
        P("fsdp", None),
        P("fsdp", None),
        P("fsdp"),
        P("fsdp"),
        P("fsdp"),
        P("fsdp"),
        P("fsdp"),
        P("fsdp"),
    )
    out_specs = (
        P(("rep", "fsdp"), "seq", None),
        P(("rep", "fsdp"), "seq", None),
        P("fsdp", None),
        P("fsdp", None),
        P("fsdp", None),
        P("fsdp", None),
        P("fsdp", None),
        P("fsdp", None),
        P("fsdp", None),
        P("fsdp"),
        P("fsdp"),
        P("fsdp"),
        P("fsdp"),
        P("fsdp"),
        P("fsdp"),
    )
    return jax.shard_map(body, mesh=mesh, in_specs=in_specs, out_specs=out_specs, check_vma=False)
```

profile of v0, /device:TPU:0, one launch (start us, length us, event | category | flops | bytes accessed | tf_op | source)
XLA Modules:
  0.0 461.6 jit_solution(1109950288446582475)
XLA Ops:
  10.4 3.0 collective-permute-start
  14.1 5.5 %all-gather.1 = bf16[2,1,1536]{2,1,0:T(2,128)(2,1)S(1)} all-gather(bf16[1,1,1536]{2,1,0:T(2,128)(2,1)S(1)} %reshape.530), channel_id=2, replica_groups=mesh['rep'=4,'fsdp'=2,'seq'=4] {'fsdp'}, dimensions={0}, use_global_device_ids=true | all-gather | bytes 9216 | tf_op jit(solution)/shard_map/all_gather | solution.py:160
  20.0 9.9 %all_gather.31 = bf16[320,1536]{1,0:T(8,128)(2,1)S(1)} all-gather(bf16[80,1536]{1,0:T(8,128)(2,1)S(1)} %collective-permute-done), channel_id=1, replica_groups=mesh['rep'=4,'fsdp'=2,'seq'=4] {'seq'}, dimensions={0}, use_global_device_ids=true | all-gather | bytes 1228800 | tf_op jit(solution)/shard_map/all_gather | solution.py:88
  36.3 8.7 %collective-permute-done.3 = bf16[256,640]{1,0:T(8,128)(2,1)S(1)} collective-permute-done((bf16[256,640]{1,0:T(8,128)(2,1)}, bf16[256,640]{1,0:T(8,128)(2,1)S(1)}, u32[]{:S(2)}, u32[]{:S(2)}) %collective-permute-start.3) | collective-permute-done | bytes 327712 | tf_op jit(solution)/shard_map/ppermute | solution.py:68
  54.6 6.8 %all_gather.33 = bf16[512,640]{1,0:T(8,128)(2,1)S(1)} all-gather(bf16[128,640]{1,0:T(8,128)(2,1)S(1)} %collective-permute-done.1), channel_id=1, replica_groups=mesh['rep'=4,'fsdp'=2,'seq'=4] {'seq'}, dimensions={0}, use_global_device_ids=true | all-gather | bytes 819200 | tf_op jit(solution)/shard_map/all_gather | solution.py:88
  63.2 5.7 %collective-permute-done.2 = bf16[80,4096]{1,0:T(8,128)(2,1)} collective-permute-done((bf16[80,4096]{1,0:T(8,128)(2,1)}, bf16[80,4096]{1,0:T(8,128)(2,1)}, u32[]{:S(2)}, u32[]{:S(2)}) %collective-permute-start.2) | collective-permute-done | bytes 655392 | tf_op jit(solution)/shard_map/ppermute | solution.py:68
  83.5 3.4 broadcast_select_fusion.3
  86.9 10.6 %all-gather.11.cloned.1.call-done = bf16[320,4096]{1,0:T(8,128)(2,1)} async-done(((bf16[80,4096]{1,0:T(8,128)(2,1)}), bf16[320,4096]{1,0:T(8,128)(2,1)}) %all-gather.11.cloned.1.call-update) | async-done | bytes 2621456 | tf_op jit(solution)/shard_map/all_gather | solution.py:88
  97.6 2.9 broadcast_select_fusion.1
  106.5 4.6 %fusion.23 = (bf16[256,2048]{1,0:T(8,128)(2,1)S(1)}, bf16[256,2048]{1,0:T(8,128)(2,1)S(1)}) fusion(f32[256,4096]{1,0:T(8,128)S(1)} %fusion.5, bf16[256,640]{1,0:T(8,128)(2,1)S(1)} %get-tuple-element.64, bf16[1024,640]{1,0:T(8,128)(2,1)S(1)} %copy-done.23, bf16[1024,640]{1,0:T(8,128)(2,1)S(1)} %copy-done.22), kind=kOutput, calls=%fused_computation.42 | convolution fusion | flops 688914432 | bytes 9240576 | tf_op jit(solution)/shard_map/dot_general | solution.py:51
  130.0 2.8 fusion.71
  132.8 12.5 %fusion.38 = bf16[1024,256]{0,1:T(8,128)(2,1)} fusion(f32[256,4,1024]{2,0,1:T(8,128)} %fusion.71, f32[256,4,1024]{2,0,1:T(8,128)} %copy-done, f32[256,4]{0,1:T(4,128)S(1)} %log_add_fusion, bf16[256,4,128]{2,0,1:T(8,128)(2,1)} %copy-done.42, bf16[256,4,128]{2,0,1:T(8,128)(2,1)} %copy-done.41), kind=kOutput, calls=%fused_computation.73 | convolution fusion | flops 545523712 | bytes 9441280 | tf_op jit(solution)/shard_map/dot_general | solution.py:57
  147.9 2.9 fusion.1
  161.7 12.3 %fusion.15 = f32[256,4,256]{2,0,1:T(8,128)} fusion(f32[256,4,1024]{2,0,1:T(8,128)} %fusion.71, f32[256,4,1024]{2,0,1:T(8,128)} %copy-done, f32[256,4]{0,1:T(4,128)S(1)} %log_add_fusion, bf16[1024,512]{1,0:T(8,128)(2,1)} %all-gather.9.cloned.1.call-done), kind=kOutput, calls=%fused_computation.33 | convolution fusion | flops 544212992 | bytes 18358272 | tf_op jit(solution)/shard_map/dot_general | solution.py:47
  177.4 5.9 %collective-permute-done.10 = bf16[2,80,4096]{2,1,0:T(8,128)(2,1)} collective-permute-done((bf16[2,80,4096]{2,1,0:T(8,128)(2,1)}, bf16[2,80,4096]{2,1,0:T(8,128)(2,1)}, u32[]{:S(2)}, u32[]{:S(2)}) %collective-permute-start.10) | collective-permute-done | bytes 1310752 | tf_op jit(solution)/shard_map/ppermute | solution.py:68
  190.4 6.9 %collective-permute-done.14 = bf16[256,640]{1,0:T(8,128)(2,1)S(1)} collective-permute-done((bf16[256,640]{1,0:T(8,128)(2,1)S(1)}, bf16[256,640]{1,0:T(8,128)(2,1)S(1)}, u32[]{:S(2)}, u32[]{:S(2)}) %collective-permute-start.14) | collective-permute-done | bytes 327712 | tf_op jit(solution)/shard_map/ppermute | solution.py:68
  198.2 5.2 %collective-permute-done.11 = bf16[80,4096]{1,0:T(8,128)(2,1)} collective-permute-done((bf16[80,4096]{1,0:T(8,128)(2,1)}, bf16[80,4096]{1,0:T(8,128)(2,1)}, u32[]{:S(2)}, u32[]{:S(2)}) %collective-permute-start.11) | collective-permute-done | bytes 655392 | tf_op jit(solution)/shard_map/ppermute | solution.py:68
  205.7 28.2 %all-reduce.10.cloned.1.call-done = bf16[256,640]{1,0:T(8,128)(2,1)} async-done(((bf16[256,640]{1,0:T(8,128)(2,1)}), bf16[256,640]{1,0:T(8,128)(2,1)}) %all-reduce.10.cloned.1.call-update) | async-done | bytes 327696 | tf_op jit(solution)/shard_map/psum | solution.py:105
  252.9 2.8 collective-permute-done.8
  256.4 20.6 %all-reduce.12.cloned.1.call-done = bf16[80,4096]{1,0:T(8,128)(2,1)} async-done(((bf16[80,4096]{1,0:T(8,128)(2,1)}), bf16[80,4096]{1,0:T(8,128)(2,1)}) %all-reduce.12.cloned.1.call-update) | async-done | bytes 655376 | tf_op jit(solution)/shard_map/psum | solution.py:105
  278.1 18.0 %all-gather.15.cloned.1.call-done = bf16[1024,640]{1,0:T(8,128)(2,1)} async-done(((bf16[256,640]{1,0:T(8,128)(2,1)}), bf16[1024,640]{1,0:T(8,128)(2,1)}) %all-gather.15.cloned.1.call-update) | async-done | bytes 1310736 | tf_op jit(solution)/shard_map/all_gather | solution.py:106
  296.1 3.0 convert_element_type.437
  299.1 34.8 %all-reduce.14.cloned.1.call-done = bf16[128,640]{1,0:T(8,128)(2,1)} async-done(((bf16[128,640]{1,0:T(8,128)(2,1)}), bf16[128,640]{1,0:T(8,128)(2,1)}) %all-reduce.14.cloned.1.call-update) | async-done | bytes 163856 | tf_op jit(solution)/shard_map/psum | solution.py:105
  333.9 2.9 fusion.59
  339.4 2.8 collective-permute-done.15
  344.1 13.9 %collective-permute-done.16 = bf16[2,96,1536]{2,1,0:T(8,128)(2,1)S(1)} collective-permute-done((bf16[2,96,1536]{2,1,0:T(8,128)(2,1)S(1)}, bf16[2,96,1536]{2,1,0:T(8,128)(2,1)S(1)}, u32[]{:S(2)}, u32[]{:S(2)}) %collective-permute-start.16) | collective-permute-done | bytes 589856 | tf_op jit(solution)/shard_map/ppermute | solution.py:68
  359.7 6.8 %collective-permute-done.17 = bf16[96,1536]{1,0:T(8,128)(2,1)S(1)} collective-permute-done((bf16[96,1536]{1,0:T(8,128)(2,1)S(1)}, bf16[96,1536]{1,0:T(8,128)(2,1)S(1)}, u32[]{:S(2)}, u32[]{:S(2)}) %collective-permute-start.17) | collective-permute-done | bytes 294944 | tf_op jit(solution)/shard_map/ppermute | solution.py:68
  368.1 35.0 %all-reduce.16.cloned.1.call-done = bf16[96,1536]{1,0:T(8,128)(2,1)} async-done(((bf16[96,1536]{1,0:T(8,128)(2,1)}), bf16[96,1536]{1,0:T(8,128)(2,1)}) %all-reduce.16.cloned.1.call-update) | async-done | bytes 294928 | tf_op jit(solution)/shard_map/psum | solution.py:105
  403.1 7.9 %all_gather.38 = bf16[512,640]{1,0:T(8,128)(2,1)S(1)} all-gather(bf16[128,640]{1,0:T(8,128)(2,1)S(1)} %copy-done.44), channel_id=1, replica_groups=mesh['rep'=4,'fsdp'=2,'seq'=4] {'seq'}, dimensions={0}, use_global_device_ids=true | all-gather | bytes 819200 | tf_op jit(solution)/shard_map/all_gather | solution.py:106
  413.1 16.9 %all-gather.19.cloned.1.call-done = bf16[320,4096]{1,0:T(8,128)(2,1)} async-done(((bf16[80,4096]{1,0:T(8,128)(2,1)}), bf16[320,4096]{1,0:T(8,128)(2,1)}) %all-gather.19.cloned.1.call-update) | async-done | bytes 2621456 | tf_op jit(solution)/shard_map/all_gather | solution.py:106
  430.0 4.8 %fusion.124 = (f32[320,2048]{1,0:T(8,128)}, f32[320,2048]{1,0:T(8,128)}) fusion(bf16[320,4096]{1,0:T(8,128)(2,1)} %all-gather.19.cloned.1.call-done), kind=kLoop, calls=%fused_computation.269 | loop fusion | bytes 10485760 | tf_op jit(solution)/shard_map/slice | solution.py:312
  434.7 14.1 %all-gather.17.cloned.1.call-done = bf16[384,1536]{1,0:T(8,128)(2,1)} async-done(((bf16[96,1536]{1,0:T(8,128)(2,1)}), bf16[384,1536]{1,0:T(8,128)(2,1)}) %all-gather.17.cloned.1.call-update) | async-done | bytes 1179664 | tf_op jit(solution)/shard_map/all_gather | solution.py:106
  (289 shorter events, 124.0 us)
Async XLA Ops:
  7.3 62.6 %all-gather.9.cloned.1.call-start = ((), (), s32[]{:S(2)}) async-start(), calls=%async_computation | async-start | bytes 1310720 | tf_op jit(solution)/shard_map/all_gather | solution.py:204
  10.4 9.5 %collective-permute-start = (bf16[80,1536]{1,0:T(8,128)(2,1)S(1)}, bf16[80,1536]{1,0:T(8,128)(2,1)S(1)}, u32[]{:S(2)}, u32[]{:S(2)}) collective-permute-start(bf16[80,1536]{1,0:T(8,128)(2,1)S(1)} %constant_dynamic-slice_fusion.5), channel_id=1, source_target_pairs={{0,4},{4,0},{1,5},{5,1},{2,6},{6,2},{3,7},{7,3},{8,12},{12,8},{9,1... | collective-permute-start | bytes 737288 | tf_op jit(solution)/shard_map/ppermute | solution.py:68
  33.0 50.5 %all-gather.13.cloned.1.call-start = ((), (), s32[]{:S(2)}) async-start(), calls=%async_computation.2 | async-start | bytes 1638400 | tf_op jit(solution)/shard_map/all_gather | solution.py:88
  34.8 10.2 %collective-permute-start.3 = (bf16[256,640]{1,0:T(8,128)(2,1)}, bf16[256,640]{1,0:T(8,128)(2,1)S(1)}, u32[]{:S(2)}, u32[]{:S(2)}) collective-permute-start(bf16[256,640]{1,0:T(8,128)(2,1)} %constant_dynamic-slice_fusion.2), channel_id=1, source_target_pairs={{0,4},{4,0},{1,5},{5,1},{2,6},{6,2},{3,7},{7,3},{8,12},{12,8},{9,1... | collective-permute-start | bytes 983048 | tf_op jit(solution)/shard_map/ppermute | solution.py:68
  45.7 51.9 %all-gather.11.cloned.1.call-start = ((), (), s32[]{:S(2)}) async-start(), calls=%async_computation.1 | async-start | bytes 3276800 | tf_op jit(solution)/shard_map/all_gather | solution.py:88
  45.8 8.8 %collective-permute-start.1 = (bf16[128,640]{1,0:T(8,128)(2,1)S(1)}, bf16[128,640]{1,0:T(8,128)(2,1)S(1)}, u32[]{:S(2)}, u32[]{:S(2)}) collective-permute-start(bf16[128,640]{1,0:T(8,128)(2,1)S(1)} %constant_dynamic-slice_fusion.4), channel_id=1, source_target_pairs={{0,4},{4,0},{1,5},{5,1},{2,6},{6,2},{3,7},{7,3},{8,12},{12,8},{9,1... | collective-permute-start | bytes 491528 | tf_op jit(solution)/shard_map/ppermute | solution.py:68
  52.7 16.3 %collective-permute-start.2 = (bf16[80,4096]{1,0:T(8,128)(2,1)}, bf16[80,4096]{1,0:T(8,128)(2,1)}, u32[]{:S(2)}, u32[]{:S(2)}) collective-permute-start(bf16[80,4096]{1,0:T(8,128)(2,1)} %constant_dynamic-slice_fusion.3), channel_id=1, source_target_pairs={{0,4},{4,0},{1,5},{5,1},{2,6},{6,2},{3,7},{7,3},{8,12},{12,8},{9,1... | collective-permute-start | bytes 1966088 | tf_op jit(solution)/shard_map/ppermute | solution.py:68
  69.0 164.9 %all-reduce.10.cloned.1.call-start = ((), (), s32[]{:S(2)}) async-start(), calls=%async_computation.3 | async-start | bytes 655360 | tf_op jit(solution)/shard_map/psum | solution.py:105
  118.9 29.0 %collective-permute-start.9 = (bf16[2,2,80,4096]{3,2,0,1:T(8,128)(2,1)}, bf16[2,2,80,4096]{3,2,0,1:T(8,128)(2,1)}, u32[]{:S(2)}, u32[]{:S(2)}) collective-permute-start(bf16[2,2,80,4096]{3,2,0,1:T(8,128)(2,1)} %bitcast.188), channel_id=1, source_target_pairs={{0,1},{1,0},{2,3},{3,2},{4,5},{5,4},{6,7},{7,6},{8,9},{9,8},{10,11... | collective-permute-start | bytes 7864328 | tf_op jit(solution)/shard_map/ppermute | solution.py:68
  125.8 115.8 %collective-permute-start.6 = (bf16[2,2,128,640]{3,2,1,0:T(8,128)(2,1)}, bf16[2,2,128,640]{3,2,1,0:T(8,128)(2,1)}, u32[]{:S(2)}, u32[]{:S(2)}) collective-permute-start(bf16[2,2,128,640]{3,2,1,0:T(8,128)(2,1)} %dynamic-slice_bitcast_fusion.4), channel_id=1, source_target_pairs={{0,1},{1,0},{2,3},{3,2},{4,5},{5,4},{6,7},{7,6},{8,9},{9,8},{10,11... | collective-permute-start | bytes 1966088 | tf_op jit(solution)/shard_map/ppermute | solution.py:68
  129.8 22.6 %collective-permute-start.12 = (bf16[2,2,256,640]{3,2,1,0:T(8,128)(2,1)}, bf16[2,2,256,640]{3,2,1,0:T(8,128)(2,1)}, u32[]{:S(2)}, u32[]{:S(2)}) collective-permute-start(bf16[2,2,256,640]{3,2,1,0:T(8,128)(2,1)} %dynamic-slice_bitcast_fusion), channel_id=1, source_target_pairs={{0,1},{1,0},{2,3},{3,2},{4,5},{5,4},{6,7},{7,6},{8,9},{9,8},{10,11... | collective-permute-start | bytes 3932168 | tf_op jit(solution)/shard_map/ppermute | solution.py:68
  152.0 31.3 %collective-permute-start.10 = (bf16[2,80,4096]{2,1,0:T(8,128)(2,1)}, bf16[2,80,4096]{2,1,0:T(8,128)(2,1)}, u32[]{:S(2)}, u32[]{:S(2)}) collective-permute-start(bf16[2,80,4096]{2,1,0:T(8,128)(2,1)} %dynamic-slice_bitcast_fusion.1), channel_id=1, source_target_pairs={{0,2},{1,3},{2,0},{3,1},{4,6},{5,7},{6,4},{7,5},{8,10},{9,11},{10,... | collective-permute-start | bytes 3932168 | tf_op jit(solution)/shard_map/ppermute | solution.py:68
  156.9 18.6 %collective-permute-start.13 = (bf16[2,256,640]{2,1,0:T(8,128)(2,1)}, bf16[2,256,640]{2,1,0:T(8,128)(2,1)}, u32[]{:S(2)}, u32[]{:S(2)}) collective-permute-start(bf16[2,256,640]{2,1,0:T(8,128)(2,1)} %dynamic-slice_bitcast_fusion.2), channel_id=1, source_target_pairs={{0,4},{4,0},{1,5},{5,1},{2,6},{6,2},{3,7},{7,3},{8,12},{12,8},{9,1... | collective-permute-start | bytes 1966088 | tf_op jit(solution)/shard_map/ppermute | solution.py:68
  187.0 16.4 %collective-permute-start.11 = (bf16[80,4096]{1,0:T(8,128)(2,1)}, bf16[80,4096]{1,0:T(8,128)(2,1)}, u32[]{:S(2)}, u32[]{:S(2)}) collective-permute-start(bf16[80,4096]{1,0:T(8,128)(2,1)} %dynamic-slice_bitcast_fusion.3), channel_id=1, source_target_pairs={{0,4},{4,0},{1,5},{5,1},{2,6},{6,2},{3,7},{7,3},{8,12},{12,8},{9,1... | collective-permute-start | bytes 1966088 | tf_op jit(solution)/shard_map/ppermute | solution.py:68
  188.5 8.8 %collective-permute-start.14 = (bf16[256,640]{1,0:T(8,128)(2,1)S(1)}, bf16[256,640]{1,0:T(8,128)(2,1)S(1)}, u32[]{:S(2)}, u32[]{:S(2)}) collective-permute-start(bf16[256,640]{1,0:T(8,128)(2,1)S(1)} %dynamic-slice_bitcast_fusion.7), channel_id=1, source_target_pairs={{0,2},{1,3},{2,0},{3,1},{4,6},{5,7},{6,4},{7,5},{8,10},{9,11},{10,... | collective-permute-start | bytes 983048 | tf_op jit(solution)/shard_map/ppermute | solution.py:68
  189.9 48.6 %collective-permute-start.4 = (bf16[2,256,512]{2,1,0:T(8,128)(2,1)}, bf16[2,256,512]{2,1,0:T(8,128)(2,1)}, u32[]{:S(2)}, u32[]{:S(2)}) collective-permute-start(bf16[2,256,512]{2,1,0:T(8,128)(2,1)} %dynamic-slice_bitcast_fusion.6), channel_id=1, source_target_pairs={{0,1},{1,0},{2,3},{3,2},{4,5},{5,4},{6,7},{7,6},{8,9},{9,8},{10,11... | collective-permute-start | bytes 1572872 | tf_op jit(solution)/shard_map/ppermute | solution.py:68
  198.1 78.8 %all-reduce.12.cloned.1.call-start = ((), (), s32[]{:S(2)}) async-start(), calls=%async_computation.4 | async-start | bytes 1310720 | tf_op jit(solution)/shard_map/psum | solution.py:105
  233.9 62.3 %all-gather.15.cloned.1.call-start = ((), (), s32[]{:S(2)}) async-start(), calls=%async_computation.6 | async-start | bytes 1638400 | tf_op jit(solution)/shard_map/all_gather | solution.py:106
  239.9 6.4 %collective-permute-start.5 = (bf16[256,512]{1,0:T(8,128)(2,1)S(1)}, bf16[256,512]{1,0:T(8,128)(2,1)S(1)}, u32[]{:S(2)}, u32[]{:S(2)}) collective-permute-start(bf16[256,512]{1,0:T(8,128)(2,1)S(1)} %dynamic-slice_bitcast_fusion.10), channel_id=1, source_target_pairs={{0,2},{1,3},{2,0},{3,1},{4,6},{5,7},{6,4},{7,5},{8,10},{9,11},{10,... | collective-permute-start | bytes 786440 | tf_op jit(solution)/shard_map/ppermute | solution.py:68
  241.5 92.4 %all-reduce.14.cloned.1.call-start = ((), (), s32[]{:S(2)}) async-start(), calls=%async_computation.5 | async-start | bytes 327680 | tf_op jit(solution)/shard_map/psum | solution.py:105
  242.9 7.3 %collective-permute-start.7 = (bf16[2,128,640]{2,1,0:T(8,128)(2,1)S(1)}, bf16[2,128,640]{2,1,0:T(8,128)(2,1)S(1)}, u32[]{:S(2)}, u32[]{:S(2)}) collective-permute-start(bf16[2,128,640]{2,1,0:T(8,128)(2,1)S(1)} %dynamic-slice_bitcast_fusion.8), channel_id=1, source_target_pairs={{0,4},{4,0},{1,5},{5,1},{2,6},{6,2},{3,7},{7,3},{8,12},{12,8},{9,1... | collective-permute-start | bytes 983048 | tf_op jit(solution)/shard_map/ppermute | solution.py:68
  250.3 5.4 %collective-permute-start.8 = (bf16[128,640]{1,0:T(8,128)(2,1)S(1)}, bf16[128,640]{1,0:T(8,128)(2,1)S(1)}, u32[]{:S(2)}, u32[]{:S(2)}) collective-permute-start(bf16[128,640]{1,0:T(8,128)(2,1)S(1)} %dynamic-slice_bitcast_fusion.11), channel_id=1, source_target_pairs={{0,2},{1,3},{2,0},{3,1},{4,6},{5,7},{6,4},{7,5},{8,10},{9,11},{10,... | collective-permute-start | bytes 491528 | tf_op jit(solution)/shard_map/ppermute | solution.py:68
  277.0 126.1 %all-reduce.16.cloned.1.call-start = ((), (), s32[]{:S(2)}) async-start(), calls=%async_computation.7 | async-start | bytes 589824 | tf_op jit(solution)/shard_map/psum | solution.py:105
  277.0 56.8 %copy-start.32 = (bf16[320,1536]{1,0:T(8,128)(2,1)S(1)}, bf16[320,1536]{1,0:T(8,128)(2,1)}, u32[]{:S(2)}) copy-start(bf16[320,1536]{1,0:T(8,128)(2,1)} %copy-done.31) | copy-start | bytes 2949124
  278.1 55.8 %copy-start.16 = (bf16[256,1536]{0,1:T(8,128)(2,1)}, bf16[256,1536]{0,1:T(8,128)(2,1)S(1)}, u32[]{:S(2)}) copy-start(bf16[256,1536]{0,1:T(8,128)(2,1)S(1)} %pad_maximum_fusion.16) | copy-start | bytes 2359300
  339.3 2.9 collective-permute-start.15
  342.6 60.5 %copy-start.44 = (bf16[128,640]{1,0:T(8,128)(2,1)S(1)}, bf16[128,640]{1,0:T(8,128)(2,1)}, u32[]{:S(2)}) copy-start(bf16[128,640]{1,0:T(8,128)(2,1)} %all-reduce.14.cloned.1.call-done) | copy-start | bytes 491524
  342.6 15.4 %collective-permute-start.16 = (bf16[2,96,1536]{2,1,0:T(8,128)(2,1)S(1)}, bf16[2,96,1536]{2,1,0:T(8,128)(2,1)S(1)}, u32[]{:S(2)}, u32[]{:S(2)}) collective-permute-start(bf16[2,96,1536]{2,1,0:T(8,128)(2,1)S(1)} %dynamic-slice_bitcast_fusion.5), channel_id=1, source_target_pairs={{0,4},{4,0},{1,5},{5,1},{2,6},{6,2},{3,7},{7,3},{8,12},{12,8},{9,1... | collective-permute-start | bytes 1769480 | tf_op jit(solution)/shard_map/ppermute | solution.py:68
  358.2 53.9 %copy-start.34 = (f32[256,640]{1,0:T(8,128)S(1)}, f32[256,640]{1,0:T(8,128)}, u32[]{:S(2)}) copy-start(f32[256,640]{1,0:T(8,128)} %get-tuple-element.89) | copy-start | bytes 1966084
  358.2 8.3 %collective-permute-start.17 = (bf16[96,1536]{1,0:T(8,128)(2,1)S(1)}, bf16[96,1536]{1,0:T(8,128)(2,1)S(1)}, u32[]{:S(2)}, u32[]{:S(2)}) collective-permute-start(bf16[96,1536]{1,0:T(8,128)(2,1)S(1)} %dynamic-slice_bitcast_fusion.9), channel_id=1, source_target_pairs={{0,2},{1,3},{2,0},{3,1},{4,6},{5,7},{6,4},{7,5},{8,10},{9,11},{10,... | collective-permute-start | bytes 884744 | tf_op jit(solution)/shard_map/ppermute | solution.py:68
  367.3 62.7 %all-gather.19.cloned.1.call-start = ((), (), s32[]{:S(2)}) async-start(), calls=%async_computation.9 | async-start | bytes 3276800 | tf_op jit(solution)/shard_map/all_gather | solution.py:106
  368.0 80.8 %all-gather.17.cloned.1.call-start = ((), (), s32[]{:S(2)}) async-start(), calls=%async_computation.8 | async-start | bytes 1474560 | tf_op jit(solution)/shard_map/all_gather | solution.py:106
  (48 other events, 334.8 us)
Sparse Core Ops, SparseCore 0:
  33.1 16.9 all-gather.8
  52.3 18.1 all-gather.12
  72.0 25.5 all-gather.10
  198.3 35.5 all-reduce.9
  236.6 40.3 all-reduce.11
  278.4 17.6 all-gather.14
  299.0 34.8 all-reduce.13
  367.4 35.6 all-reduce.15
  404.7 25.2 all-gather.18
  431.4 17.4 all-gather.16
where the time goes:
time: 470 us; the launch traced here: 462 us
  waiting for transfers between devices  242 us (51%)
  matrix products  57.4 us (12%)
  local copies, waits for them, and re-layouts  50.7 us (11%)
  other arithmetic  47.7 us (10%)
  blocking collectives  30.1 us (6%)
  starting transfers between devices  18.4 us (4%)
  between operations  15.4 us (3%)
    psum x4, waiting for transfers between devices, reduce_blocks(): part = lax.psum(part, 'rep')  118 us
    ppermute x18, waiting for transfers between devices, swap(): return lax.ppermute(values, axis_name, [(i, i ^ bit) for i in range(size)])  62.7 us
    all_gather x3, waiting for transfers between devices, reduce_blocks(): lax.all_gather(part, 'seq', axis=0, tiled=True).reshape(4, rows, columns)  49 us
    dot_general x6, matrix products, transpose_times(): lax.dot_general(left_side, right_side, (((0,), (0,)), ((), ())), preferre...  21.6 us
    dot_general x6, matrix products, matmul(): return jnp.dot(left_side, right_side, preferred_element_type=jnp.float32)  20.7 us
    ppermute x18, starting transfers between devices, swap(): return lax.ppermute(values, axis_name, [(i, i ^ bit) for i in range(size)])  18 us
    all_gather x2, blocking collectives, gather_rows(): other = lax.all_gather(swap(piece, 'fsdp', 1), 'seq', axis=0, tiled=True)  16.8 us
    convert_element_type x13, other arithmetic, halve(): (kept.astype(jnp.float32) + arrived.astype(jnp.float32)).astype(jnp.bfloa...  15.8 us
  transfers between devices with their start and end apart: 28, of which 19 were waited for; matrix products, arithmetic and copies ran while one was open for 23% of the time, Pallas kernels for 0%

commit v1 on v0

--- a/solution.py
+++ b/solution.py
@@ -102,7 +102,7 @@
         part = halve(part, "fsdp", 1, 0)
     if before is not None:
         part, _ = lax.optimization_barrier((part, before))
-    part = lax.psum(part, "rep")
+    part = jnp.sum(jax.lax.all_gather(part, "rep"), axis=0)
     return (lax.all_gather(part, "seq", axis=0, tiled=True).reshape(4, rows, columns), part)
 
 

time: 470 us -> 426 us (0.906)
  waiting for transfers between devices: 242 us -> 168 us
  blocking collectives: 30.1 us -> 47.3 us
  other arithmetic: 47.7 us -> 56.5 us
  matrix products: 57.4 us -> 62.8 us
    psum x4 -> x0, waiting for transfers between devices: 118 us -> none  [reduce_blocks(): part = lax.psum(part, 'rep')]
    all_gather x0 -> x3, waiting for transfers between devices: none -> 38.7 us  [reduce_blocks(): part = jnp.sum(jax.lax.all_gather(part, 'rep'), axis=0)]
    ppermute x18, waiting for transfers between devices: 62.7 us -> 93.9 us  [swap(): return lax.ppermute(values, axis_name, [(i, i ^ bit) for i in range(size)])]
    all_gather x3, waiting for transfers between devices: 49 us -> 29.5 us  [reduce_blocks(): lax.all_gather(part, 'seq', axis=0, tiled=True).reshape(4, rows, columns)]
    all_gather x0 -> x1, blocking collectives: none -> 17.1 us  [reduce_blocks(): part = jnp.sum(jax.lax.all_gather(part, 'rep'), axis=0)]
    reduce_sum x0 -> x4, other arithmetic: none -> 8.56 us  [reduce_blocks(): part = jnp.sum(jax.lax.all_gather(part, 'rep'), axis=0)]
    all_gather x2, waiting for transfers between devices: 10.7 us -> 5.33 us  [gather_rows(): other = lax.all_gather(swap(piece, 'fsdp', 1), 'seq', axis=0, tiled=True)]
    squeeze x12 -> x13, local copies, waits for them, and re-layouts: 6.2 us -> 10.4 us  [halve(): sent = lax.dynamic_index_in_dim(values, 1 - mine, dim, keepdims=False)]
  transfers between devices with their start and end apart: 28 -> 27, of which waited for: 19 -> 17; matrix products, arithmetic and copies ran while one was open for 23% -> 29% of each run, Pallas kernels for 0% -> 0%
where the time goes in v1:
time: 426 us; the launch traced here: 418 us
  waiting for transfers between devices  168 us (39%)
  matrix products  62.8 us (15%)
  other arithmetic  56.5 us (13%)
  local copies, waits for them, and re-layouts  49.3 us (12%)
  blocking collectives  47.3 us (11%)
  starting transfers between devices  18.3 us (4%)
  between operations  15.2 us (4%)
    ppermute x18, waiting for transfers between devices, swap(): return lax.ppermute(values, axis_name, [(i, i ^ bit) for i in range(size)])  93.9 us
    all_gather x3, waiting for transfers between devices, reduce_blocks(): part = jnp.sum(jax.lax.all_gather(part, 'rep'), axis=0)  38.7 us
    all_gather x3, waiting for transfers between devices, reduce_blocks(): lax.all_gather(part, 'seq', axis=0, tiled=True).reshape(4, rows, columns)  29.5 us
    dot_general x6, matrix products, transpose_times(): lax.dot_general(left_side, right_side, (((0,), (0,)), ((), ())), preferre...  21.9 us
    dot_general x6, matrix products, matmul(): return jnp.dot(left_side, right_side, preferred_element_type=jnp.float32)  21.1 us
    dot_general x6, matrix products, times_transpose(): lax.dot_general(left_side, right_side, (((1,), (1,)), ((), ())), preferre...  19.7 us
    ppermute x18, starting transfers between devices, swap(): return lax.ppermute(values, axis_name, [(i, i ^ bit) for i in range(size)])  17.7 us
    all_gather x1, blocking collectives, reduce_blocks(): part = jnp.sum(jax.lax.all_gather(part, 'rep'), axis=0)  17.1 us
  transfers between devices with their start and end apart: 27, of which 17 were waited for; matrix products, arithmetic and copies ran while one was open for 29% of the time, Pallas kernels for 0%

profile of v1, /device:TPU:0, one launch (start us, length us, event | category | flops | bytes accessed | tf_op | source)
XLA Modules:
  0.0 417.8 jit_solution(5455220448694508002)
XLA Ops:
  10.4 3.0 collective-permute-start
  14.1 5.5 %all-gather.5 = bf16[2,1,1536]{2,1,0:T(2,128)(2,1)S(1)} all-gather(bf16[1,1,1536]{2,1,0:T(2,128)(2,1)S(1)} %reshape.534), channel_id=2, replica_groups=mesh['rep'=4,'fsdp'=2,'seq'=4] {'fsdp'}, dimensions={0}, use_global_device_ids=true | all-gather | bytes 9216 | tf_op jit(solution)/shard_map/all_gather | solution.py:160
  20.0 9.9 %all_gather.55 = bf16[320,1536]{1,0:T(8,128)(2,1)S(1)} all-gather(bf16[80,1536]{1,0:T(8,128)(2,1)S(1)} %collective-permute-done), channel_id=1, replica_groups=mesh['rep'=4,'fsdp'=2,'seq'=4] {'seq'}, dimensions={0}, use_global_device_ids=true | all-gather | bytes 1228800 | tf_op jit(solution)/shard_map/all_gather | solution.py:88
  35.6 8.5 %collective-permute-done.3 = bf16[256,640]{1,0:T(8,128)(2,1)S(1)} collective-permute-done((bf16[256,640]{1,0:T(8,128)(2,1)S(1)}, bf16[256,640]{1,0:T(8,128)(2,1)S(1)}, u32[]{:S(2)}, u32[]{:S(2)}) %collective-permute-start.3) | collective-permute-done | bytes 327712 | tf_op jit(solution)/shard_map/ppermute | solution.py:68
  54.6 15.4 %collective-permute-done.1 = bf16[128,640]{1,0:T(8,128)(2,1)S(1)} collective-permute-done((bf16[128,640]{1,0:T(8,128)(2,1)S(1)}, bf16[128,640]{1,0:T(8,128)(2,1)S(1)}, u32[]{:S(2)}, u32[]{:S(2)}) %collective-permute-start.1) | collective-permute-done | bytes 163872 | tf_op jit(solution)/shard_map/ppermute | solution.py:68
  70.1 6.8 %all_gather.57 = bf16[512,640]{1,0:T(8,128)(2,1)S(1)} all-gather(bf16[128,640]{1,0:T(8,128)(2,1)S(1)} %collective-permute-done.1), channel_id=1, replica_groups=mesh['rep'=4,'fsdp'=2,'seq'=4] {'seq'}, dimensions={0}, use_global_device_ids=true | all-gather | bytes 819200 | tf_op jit(solution)/shard_map/all_gather | solution.py:88
  95.3 3.4 broadcast_select_fusion.3
  98.7 5.3 %all-gather.18.cloned.1.call-done = bf16[320,4096]{1,0:T(8,128)(2,1)} async-done(((bf16[80,4096]{1,0:T(8,128)(2,1)}), bf16[320,4096]{1,0:T(8,128)(2,1)}) %all-gather.18.cloned.1.call-update) | async-done | bytes 2621456 | tf_op jit(solution)/shard_map/all_gather | solution.py:88
  104.0 2.9 broadcast_select_fusion.1
  113.4 4.6 %fusion.23 = (bf16[256,2048]{1,0:T(8,128)(2,1)S(1)}, bf16[256,2048]{1,0:T(8,128)(2,1)S(1)}) fusion(f32[256,4096]{1,0:T(8,128)S(1)} %fusion.5, bf16[256,640]{1,0:T(8,128)(2,1)S(1)} %get-tuple-element.62, bf16[1024,640]{1,0:T(8,128)(2,1)S(1)} %copy-done.22, bf16[1024,640]{1,0:T(8,128)(2,1)S(1)} %copy-done.21), kind=kOutput, calls=%fused_computation.41 | convolution fusion | flops 688914432 | bytes 9240576 | tf_op jit(solution)/shard_map/dot_general | solution.py:51
  126.0 5.2 %multiply_reduce_fusion.3 = (bf16[640]{0:T(1024)(128)(2,1)S(1)}, f32[256]{0:T(256)S(1)}, f32[256,640]{1,0:T(8,128)S(1)}) fusion(f32[256,640]{1,0:T(8,128)S(1)} %get-tuple-element.43, f32[256]{0:T(256)S(1)} %fusion.102, f32[640]{0:T(1024)S(1)} %reshape.511, bf16[320,4096]{1,0:T(8,128)(2,1)} %copy-done.16, bf16[320,4096]{1,0:T(8,128)(2,1)} %copy-done.15, ...), kind=kOutput, calls=%fused_computation.128 | convolution fusion | flops 1357839488 | bytes 8656640 | tf_op jit(solution)/shard_map/dot_general | solution.py:51
  135.0 15.0 %collective-permute-done.13 = bf16[2,256,640]{2,1,0:T(8,128)(2,1)S(1)} collective-permute-done((bf16[2,256,640]{2,1,0:T(8,128)(2,1)S(1)}, bf16[2,256,640]{2,1,0:T(8,128)(2,1)S(1)}, u32[]{:S(2)}, u32[]{:S(2)}) %collective-permute-start.13) | collective-permute-done | bytes 655392 | tf_op jit(solution)/shard_map/ppermute | solution.py:68
  157.3 3.6 collective-permute-done.14
  171.2 16.3 %collective-permute-done.10 = bf16[2,80,4096]{2,1,0:T(8,128)(2,1)} collective-permute-done((bf16[2,80,4096]{2,1,0:T(8,128)(2,1)}, bf16[2,80,4096]{2,1,0:T(8,128)(2,1)}, u32[]{:S(2)}, u32[]{:S(2)}) %collective-permute-start.10) | collective-permute-done | bytes 1310752 | tf_op jit(solution)/shard_map/ppermute | solution.py:68
  190.3 4.1 all-gather.28.cloned.1.call-done
  200.4 12.9 %fusion.38 = bf16[1024,256]{0,1:T(8,128)(2,1)} fusion(f32[256,4,1024]{2,0,1:T(8,128)} %fusion.71, f32[256,4,1024]{2,0,1:T(8,128)} %copy-done.2, f32[256,4]{0,1:T(4,128)S(1)} %log_add_fusion, bf16[256,4,128]{2,0,1:T(8,128)(2,1)} %copy-done.37, bf16[256,4,128]{2,0,1:T(8,128)(2,1)} %copy-done.36), kind=kOutput, calls=%fused_computation.72 | convolution fusion | flops 545523712 | bytes 9441280 | tf_op jit(solution)/shard_map/dot_general | solution.py:57
  223.4 13.0 %fusion.15 = f32[256,4,256]{2,0,1:T(8,128)} fusion(f32[256,4,1024]{2,0,1:T(8,128)} %fusion.71, f32[256,4,1024]{2,0,1:T(8,128)} %copy-done.2, f32[256,4]{0,1:T(4,128)S(1)} %log_add_fusion, bf16[1024,512]{1,0:T(8,128)(2,1)} %all-gather.16.cloned.1.call-done), kind=kOutput, calls=%fused_computation.32 | convolution fusion | flops 544212992 | bytes 18358272 | tf_op jit(solution)/shard_map/dot_general | solution.py:47
  248.9 4.8 %collective-permute-done.5 = bf16[256,512]{1,0:T(8,128)(2,1)S(1)} collective-permute-done((bf16[256,512]{1,0:T(8,128)(2,1)S(1)}, bf16[256,512]{1,0:T(8,128)(2,1)S(1)}, u32[]{:S(2)}, u32[]{:S(2)}) %collective-permute-start.5) | collective-permute-done | bytes 262176 | tf_op jit(solution)/shard_map/ppermute | solution.py:68
  260.5 4.8 %collective-permute-done.8 = bf16[128,640]{1,0:T(8,128)(2,1)S(1)} collective-permute-done((bf16[128,640]{1,0:T(8,128)(2,1)S(1)}, bf16[128,640]{1,0:T(8,128)(2,1)S(1)}, u32[]{:S(2)}, u32[]{:S(2)}) %collective-permute-start.8) | collective-permute-done | bytes 163872 | tf_op jit(solution)/shard_map/ppermute | solution.py:68
  265.4 3.0 convert_element_type.445
  268.3 6.2 %all-gather.30.cloned.1.call-done = bf16[320,4096]{1,0:T(8,128)(2,1)} async-done(((bf16[80,4096]{1,0:T(8,128)(2,1)}), bf16[320,4096]{1,0:T(8,128)(2,1)}) %all-gather.30.cloned.1.call-update) | async-done | bytes 2621456 | tf_op jit(solution)/shard_map/all_gather | solution.py:105
  274.6 3.2 reduce_sum.310
  277.8 17.1 %all-gather.3 = bf16[512,640]{1,0:T(8,128)(2,1)S(1)} all-gather(bf16[128,640]{1,0:T(8,128)(2,1)S(1)} %fusion.80), channel_id=5, replica_groups=mesh['rep'=4,'fsdp'=2,'seq'=4] {'rep'}, dimensions={0}, use_global_device_ids=true | all-gather | bytes 819200 | tf_op jit(solution)/shard_map/all_gather | solution.py:105
  295.7 3.2 fusion.59
  301.5 2.8 collective-permute-done.15
  306.1 14.0 %collective-permute-done.16 = bf16[2,96,1536]{2,1,0:T(8,128)(2,1)S(1)} collective-permute-done((bf16[2,96,1536]{2,1,0:T(8,128)(2,1)S(1)}, bf16[2,96,1536]{2,1,0:T(8,128)(2,1)S(1)}, u32[]{:S(2)}, u32[]{:S(2)}) %collective-permute-start.16) | collective-permute-done | bytes 589856 | tf_op jit(solution)/shard_map/ppermute | solution.py:68
  321.8 6.8 %collective-permute-done.17 = bf16[96,1536]{1,0:T(8,128)(2,1)S(1)} collective-permute-done((bf16[96,1536]{1,0:T(8,128)(2,1)S(1)}, bf16[96,1536]{1,0:T(8,128)(2,1)S(1)}, u32[]{:S(2)}, u32[]{:S(2)}) %collective-permute-start.17) | collective-permute-done | bytes 294944 | tf_op jit(solution)/shard_map/ppermute | solution.py:68
  330.2 28.4 %all-gather.32.cloned.1.call-done = bf16[384,1536]{1,0:T(8,128)(2,1)} async-done(((bf16[96,1536]{1,0:T(8,128)(2,1)}), bf16[384,1536]{1,0:T(8,128)(2,1)}) %all-gather.32.cloned.1.call-update) | async-done | bytes 1179664 | tf_op jit(solution)/shard_map/all_gather | solution.py:105
  361.0 7.9 %all_gather.70 = bf16[512,640]{1,0:T(8,128)(2,1)S(1)} all-gather(bf16[128,640]{1,0:T(8,128)(2,1)S(1)} %copy-done.32), channel_id=1, replica_groups=mesh['rep'=4,'fsdp'=2,'seq'=4] {'seq'}, dimensions={0}, use_global_device_ids=true | all-gather | bytes 819200 | tf_op jit(solution)/shard_map/all_gather | solution.py:106
  371.0 14.6 %all-gather.26.cloned.1.call-done = bf16[320,4096]{1,0:T(8,128)(2,1)} async-done(((bf16[80,4096]{1,0:T(8,128)(2,1)}), bf16[320,4096]{1,0:T(8,128)(2,1)}) %all-gather.26.cloned.1.call-update) | async-done | bytes 2621456 | tf_op jit(solution)/shard_map/all_gather | solution.py:106
  385.6 4.8 %fusion.124 = (f32[320,2048]{1,0:T(8,128)}, f32[320,2048]{1,0:T(8,128)}) fusion(bf16[320,4096]{1,0:T(8,128)(2,1)} %all-gather.26.cloned.1.call-done), kind=kLoop, calls=%fused_computation.266 | loop fusion | bytes 10485760 | tf_op jit(solution)/shard_map/slice | solution.py:312
  390.3 14.9 %all-gather.24.cloned.1.call-done = bf16[384,1536]{1,0:T(8,128)(2,1)} async-done(((bf16[96,1536]{1,0:T(8,128)(2,1)}), bf16[384,1536]{1,0:T(8,128)(2,1)}) %all-gather.24.cloned.1.call-update) | async-done | bytes 1179664 | tf_op jit(solution)/shard_map/all_gather | solution.py:106
  (278 shorter events, 130.4 us)
Async XLA Ops:
  7.3 73.5 %all-gather.16.cloned.1.call-start = ((), (), s32[]{:S(2)}) async-start(), calls=%async_computation | async-start | bytes 1310720 | tf_op jit(solution)/shard_map/all_gather | solution.py:204
  10.4 9.5 %collective-permute-start = (bf16[80,1536]{1,0:T(8,128)(2,1)S(1)}, bf16[80,1536]{1,0:T(8,128)(2,1)S(1)}, u32[]{:S(2)}, u32[]{:S(2)}) collective-permute-start(bf16[80,1536]{1,0:T(8,128)(2,1)S(1)} %constant_dynamic-slice_fusion.3), channel_id=1, source_target_pairs={{0,4},{4,0},{1,5},{5,1},{2,6},{6,2},{3,7},{7,3},{8,12},{12,8},{9,1... | collective-permute-start | bytes 737288 | tf_op jit(solution)/shard_map/ppermute | solution.py:68
  31.3 48.0 %copy-start.11 = (f32[256,1536]{1,0:T(8,128)}, f32[256,1536]{1,0:T(8,128)S(1)}, u32[]{:S(2)}) copy-start(f32[256,1536]{1,0:T(8,128)S(1)} %fusion.42) | copy-start | bytes 4718596
  32.2 48.4 %copy-start.23 = (f32[256,128]{1,0:T(8,128)}, f32[256,128]{1,0:T(8,128)S(1)}, u32[]{:S(2)}) copy-start(f32[256,128]{1,0:T(8,128)S(1)} %get-tuple-element.76) | copy-start | bytes 393220
  32.2 48.4 %copy-start.25 = (f32[256,128]{1,0:T(8,128)}, f32[256,128]{1,0:T(8,128)S(1)}, u32[]{:S(2)}) copy-start(f32[256,128]{1,0:T(8,128)S(1)} %get-tuple-element.77) | copy-start | bytes 393220
  33.0 62.3 %all-gather.20.cloned.1.call-start = ((), (), s32[]{:S(2)}) async-start(), calls=%async_computation.2 | async-start | bytes 1638400 | tf_op jit(solution)/shard_map/all_gather | solution.py:88
  34.1 10.0 %collective-permute-start.3 = (bf16[256,640]{1,0:T(8,128)(2,1)S(1)}, bf16[256,640]{1,0:T(8,128)(2,1)S(1)}, u32[]{:S(2)}, u32[]{:S(2)}) collective-permute-start(bf16[256,640]{1,0:T(8,128)(2,1)S(1)} %constant_dynamic-slice_fusion), channel_id=1, source_target_pairs={{0,4},{4,0},{1,5},{5,1},{2,6},{6,2},{3,7},{7,3},{8,12},{12,8},{9,1... | collective-permute-start | bytes 983048 | tf_op jit(solution)/shard_map/ppermute | solution.py:68
  44.8 59.2 %all-gather.18.cloned.1.call-start = ((), (), s32[]{:S(2)}) async-start(), calls=%async_computation.1 | async-start | bytes 3276800 | tf_op jit(solution)/shard_map/all_gather | solution.py:88
  50.2 26.7 %collective-permute-start.2 = (bf16[80,4096]{1,0:T(8,128)(2,1)}, bf16[80,4096]{1,0:T(8,128)(2,1)}, u32[]{:S(2)}, u32[]{:S(2)}) collective-permute-start(bf16[80,4096]{1,0:T(8,128)(2,1)} %constant_dynamic-slice_fusion.1), channel_id=1, source_target_pairs={{0,4},{4,0},{1,5},{5,1},{2,6},{6,2},{3,7},{7,3},{8,12},{12,8},{9,1... | collective-permute-start | bytes 1966088 | tf_op jit(solution)/shard_map/ppermute | solution.py:68
  52.6 17.4 %collective-permute-start.1 = (bf16[128,640]{1,0:T(8,128)(2,1)S(1)}, bf16[128,640]{1,0:T(8,128)(2,1)S(1)}, u32[]{:S(2)}, u32[]{:S(2)}) collective-permute-start(bf16[128,640]{1,0:T(8,128)(2,1)S(1)} %constant_dynamic-slice_fusion.2), channel_id=1, source_target_pairs={{0,4},{4,0},{1,5},{5,1},{2,6},{6,2},{3,7},{7,3},{8,12},{12,8},{9,1... | collective-permute-start | bytes 491528 | tf_op jit(solution)/shard_map/ppermute | solution.py:68
  76.9 117.4 %all-gather.28.cloned.1.call-start = ((), (), s32[]{:S(2)}) async-start(), calls=%async_computation.6 | async-start | bytes 1638400 | tf_op jit(solution)/shard_map/all_gather | solution.py:105
  120.4 10.9 %collective-permute-start.12 = (bf16[2,2,256,640]{3,2,1,0:T(8,128)(2,1)}, bf16[2,2,256,640]{3,2,1,0:T(8,128)(2,1)}, u32[]{:S(2)}, u32[]{:S(2)}) collective-permute-start(bf16[2,2,256,640]{3,2,1,0:T(8,128)(2,1)} %dynamic-slice_bitcast_fusion.1), channel_id=1, source_target_pairs={{0,1},{1,0},{2,3},{3,2},{4,5},{5,4},{6,7},{7,6},{8,9},{9,8},{10,11... | collective-permute-start | bytes 3932168 | tf_op jit(solution)/shard_map/ppermute | solution.py:68
  125.7 24.9 %collective-permute-start.9 = (bf16[2,2,80,4096]{3,2,1,0:T(8,128)(2,1)}, bf16[2,2,80,4096]{3,2,1,0:T(8,128)(2,1)}, u32[]{:S(2)}, u32[]{:S(2)}) collective-permute-start(bf16[2,2,80,4096]{3,2,1,0:T(8,128)(2,1)} %dynamic-slice_bitcast_fusion), channel_id=1, source_target_pairs={{0,1},{1,0},{2,3},{3,2},{4,5},{5,4},{6,7},{7,6},{8,9},{9,8},{10,11... | collective-permute-start | bytes 7864328 | tf_op jit(solution)/shard_map/ppermute | solution.py:68
  133.0 17.0 %collective-permute-start.13 = (bf16[2,256,640]{2,1,0:T(8,128)(2,1)S(1)}, bf16[2,256,640]{2,1,0:T(8,128)(2,1)S(1)}, u32[]{:S(2)}, u32[]{:S(2)}) collective-permute-start(bf16[2,256,640]{2,1,0:T(8,128)(2,1)S(1)} %dynamic-slice_bitcast_fusion.3), channel_id=1, source_target_pairs={{0,4},{4,0},{1,5},{5,1},{2,6},{6,2},{3,7},{7,3},{8,12},{12,8},{9,1... | collective-permute-start | bytes 1966088 | tf_op jit(solution)/shard_map/ppermute | solution.py:68
  150.2 10.6 %collective-permute-start.14 = (bf16[256,640]{1,0:T(8,128)(2,1)S(1)}, bf16[256,640]{1,0:T(8,128)(2,1)S(1)}, u32[]{:S(2)}, u32[]{:S(2)}) collective-permute-start(bf16[256,640]{1,0:T(8,128)(2,1)S(1)} %dynamic-slice_bitcast_fusion.8), channel_id=1, source_target_pairs={{0,2},{1,3},{2,0},{3,1},{4,6},{5,7},{6,4},{7,5},{8,10},{9,11},{10,... | collective-permute-start | bytes 983048 | tf_op jit(solution)/shard_map/ppermute | solution.py:68
  154.7 32.8 %collective-permute-start.10 = (bf16[2,80,4096]{2,1,0:T(8,128)(2,1)}, bf16[2,80,4096]{2,1,0:T(8,128)(2,1)}, u32[]{:S(2)}, u32[]{:S(2)}) collective-permute-start(bf16[2,80,4096]{2,1,0:T(8,128)(2,1)} %dynamic-slice_bitcast_fusion.2), channel_id=1, source_target_pairs={{0,2},{1,3},{2,0},{3,1},{4,6},{5,7},{6,4},{7,5},{8,10},{9,11},{10,... | collective-permute-start | bytes 3932168 | tf_op jit(solution)/shard_map/ppermute | solution.py:68
  161.7 103.7 %all-gather.22.cloned.1.call-start = ((), (), s32[]{:S(2)}) async-start(), calls=%async_computation.3 | async-start | bytes 1638400 | tf_op jit(solution)/shard_map/all_gather | solution.py:106
  168.4 78.1 %collective-permute-start.6 = (bf16[2,2,128,640]{3,2,1,0:T(8,128)(2,1)}, bf16[2,2,128,640]{3,2,1,0:T(8,128)(2,1)}, u32[]{:S(2)}, u32[]{:S(2)}) collective-permute-start(bf16[2,2,128,640]{3,2,1,0:T(8,128)(2,1)} %dynamic-slice_bitcast_fusion.5), channel_id=1, source_target_pairs={{0,1},{1,0},{2,3},{3,2},{4,5},{5,4},{6,7},{7,6},{8,9},{9,8},{10,11... | collective-permute-start | bytes 1966088 | tf_op jit(solution)/shard_map/ppermute | solution.py:68
  196.7 77.9 %all-gather.30.cloned.1.call-start = ((), (), s32[]{:S(2)}) async-start(), calls=%async_computation.7 | async-start | bytes 3276800 | tf_op jit(solution)/shard_map/all_gather | solution.py:105
  199.0 20.2 %collective-permute-start.11 = (bf16[80,4096]{1,0:T(8,128)(2,1)}, bf16[80,4096]{1,0:T(8,128)(2,1)}, u32[]{:S(2)}, u32[]{:S(2)}) collective-permute-start(bf16[80,4096]{1,0:T(8,128)(2,1)} %dynamic-slice_bitcast_fusion.4), channel_id=1, source_target_pairs={{0,4},{4,0},{1,5},{5,1},{2,6},{6,2},{3,7},{7,3},{8,12},{12,8},{9,1... | collective-permute-start | bytes 1966088 | tf_op jit(solution)/shard_map/ppermute | solution.py:68
  221.5 137.1 %all-gather.32.cloned.1.call-start = ((), (), s32[]{:S(2)}) async-start(), calls=%async_computation.8 | async-start | bytes 1474560 | tf_op jit(solution)/shard_map/all_gather | solution.py:105
  223.4 20.3 %collective-permute-start.4 = (bf16[2,256,512]{2,1,0:T(8,128)(2,1)}, bf16[2,256,512]{2,1,0:T(8,128)(2,1)}, u32[]{:S(2)}, u32[]{:S(2)}) collective-permute-start(bf16[2,256,512]{2,1,0:T(8,128)(2,1)} %dynamic-slice_bitcast_fusion.7), channel_id=1, source_target_pairs={{0,1},{1,0},{2,3},{3,2},{4,5},{5,4},{6,7},{7,6},{8,9},{9,8},{10,11... | collective-permute-start | bytes 1572872 | tf_op jit(solution)/shard_map/ppermute | solution.py:68
  245.1 8.7 %collective-permute-start.5 = (bf16[256,512]{1,0:T(8,128)(2,1)S(1)}, bf16[256,512]{1,0:T(8,128)(2,1)S(1)}, u32[]{:S(2)}, u32[]{:S(2)}) collective-permute-start(bf16[256,512]{1,0:T(8,128)(2,1)S(1)} %dynamic-slice_bitcast_fusion.11), channel_id=1, source_target_pairs={{0,2},{1,3},{2,0},{3,1},{4,6},{5,7},{6,4},{7,5},{8,10},{9,11},{10,... | collective-permute-start | bytes 786440 | tf_op jit(solution)/shard_map/ppermute | solution.py:68
  248.6 10.1 %collective-permute-start.7 = (bf16[2,128,640]{2,1,0:T(8,128)(2,1)}, bf16[2,128,640]{2,1,0:T(8,128)(2,1)}, u32[]{:S(2)}, u32[]{:S(2)}) collective-permute-start(bf16[2,128,640]{2,1,0:T(8,128)(2,1)} %dynamic-slice_bitcast_fusion.9), channel_id=1, source_target_pairs={{0,4},{4,0},{1,5},{5,1},{2,6},{6,2},{3,7},{7,3},{8,12},{12,8},{9,1... | collective-permute-start | bytes 983048 | tf_op jit(solution)/shard_map/ppermute | solution.py:68
  259.8 5.5 %collective-permute-start.8 = (bf16[128,640]{1,0:T(8,128)(2,1)S(1)}, bf16[128,640]{1,0:T(8,128)(2,1)S(1)}, u32[]{:S(2)}, u32[]{:S(2)}) collective-permute-start(bf16[128,640]{1,0:T(8,128)(2,1)S(1)} %dynamic-slice_bitcast_fusion.12), channel_id=1, source_target_pairs={{0,2},{1,3},{2,0},{3,1},{4,6},{5,7},{6,4},{7,5},{8,10},{9,11},{10,... | collective-permute-start | bytes 491528 | tf_op jit(solution)/shard_map/ppermute | solution.py:68
  260.5 35.2 %copy-start.12 = (bf16[256,1536]{0,1:T(8,128)(2,1)}, bf16[256,1536]{0,1:T(8,128)(2,1)S(1)}, u32[]{:S(2)}) copy-start(bf16[256,1536]{0,1:T(8,128)(2,1)S(1)} %pad_maximum_fusion.16) | copy-start | bytes 2359300
  301.4 2.9 collective-permute-start.15
  304.7 15.4 %collective-permute-start.16 = (bf16[2,96,1536]{2,1,0:T(8,128)(2,1)S(1)}, bf16[2,96,1536]{2,1,0:T(8,128)(2,1)S(1)}, u32[]{:S(2)}, u32[]{:S(2)}) collective-permute-start(bf16[2,96,1536]{2,1,0:T(8,128)(2,1)S(1)} %dynamic-slice_bitcast_fusion.6), channel_id=1, source_target_pairs={{0,4},{4,0},{1,5},{5,1},{2,6},{6,2},{3,7},{7,3},{8,12},{12,8},{9,1... | collective-permute-start | bytes 1769480 | tf_op jit(solution)/shard_map/ppermute | solution.py:68
  320.3 40.6 %copy-start.32 = (bf16[128,640]{1,0:T(8,128)(2,1)S(1)}, bf16[128,640]{1,0:T(8,128)(2,1)}, u32[]{:S(2)}) copy-start(bf16[128,640]{1,0:T(8,128)(2,1)} %reduce_sum.311) | copy-start | bytes 491524
  320.4 8.3 %collective-permute-start.17 = (bf16[96,1536]{1,0:T(8,128)(2,1)S(1)}, bf16[96,1536]{1,0:T(8,128)(2,1)S(1)}, u32[]{:S(2)}, u32[]{:S(2)}) collective-permute-start(bf16[96,1536]{1,0:T(8,128)(2,1)S(1)} %dynamic-slice_bitcast_fusion.10), channel_id=1, source_target_pairs={{0,2},{1,3},{2,0},{3,1},{4,6},{5,7},{6,4},{7,5},{8,10},{9,11},{10,... | collective-permute-start | bytes 884744 | tf_op jit(solution)/shard_map/ppermute | solution.py:68
  329.4 56.1 %all-gather.26.cloned.1.call-start = ((), (), s32[]{:S(2)}) async-start(), calls=%async_computation.5 | async-start | bytes 3276800 | tf_op jit(solution)/shard_map/all_gather | solution.py:106
  330.2 75.0 %all-gather.24.cloned.1.call-start = ((), (), s32[]{:S(2)}) async-start(), calls=%async_computation.4 | async-start | bytes 1474560 | tf_op jit(solution)/shard_map/all_gather | solution.py:106
  (41 other events, 179.5 us)
Sparse Core Ops, SparseCore 0:
  33.1 16.9 all-gather.15
  52.3 18.1 all-gather.19
  77.1 26.9 all-gather.17
  161.8 32.5 all-gather.27
  196.8 17.2 all-gather.21
  221.6 52.9 all-gather.29
  329.5 29.0 all-gather.31
  360.8 24.7 all-gather.25
  387.7 17.4 all-gather.23
